TPU v7x, 32 devices: a whole 2x2x4 slice. The times are simulated.
32 devices in a mesh: shard: 16 (over z, x, core), rep: 2 (over y).
Axes of the slice: x: 2, y: 2, z: 4, core: 2. Of those that a mesh axis runs over, the one named last changes fastest.
Arguments:
- frames: bfloat16 [32, 256, 768], P(('shard', 'rep')), may hold values from -6 to 6
- cotangent: bfloat16 [32, 256, 768], P(('shard', 'rep')), may hold values from -6 to 6
- first_gain: bfloat16 [768], P('shard'), may hold values from 0.5 to 1.5
- first_shift: bfloat16 [768], P('shard'), may hold values from -1.75 to 1.75
- query_weight: bfloat16 [768, 768], P('shard'), may hold values from -0.21875 to 0.21875
- query_bias: bfloat16 [768], P('shard'), may hold values from -1.75 to 1.75
- key_weight: bfloat16 [768, 768], P('shard'), may hold values from -0.21875 to 0.21875
- value_weight: bfloat16 [768, 768], P('shard'), may hold values from -0.21875 to 0.21875
- value_bias: bfloat16 [768], P('shard'), may hold values from -1.75 to 1.75
- output_weight: bfloat16 [768, 768], P('shard'), may hold values from -0.4375 to 0.4375
- output_bias: bfloat16 [768], P('shard'), may hold values from -1.75 to 1.75
- second_gain: bfloat16 [768], P('shard'), may hold values from 0.5 to 1.5
- second_shift: bfloat16 [768], P('shard'), may hold values from -1.75 to 1.75
- inner_weight: bfloat16 [768, 3072], P('shard'), may hold values from -0.21875 to 0.21875
- inner_bias: bfloat16 [3072], P('shard'), may hold values from -1.75 to 1.75
- outer_weight: bfloat16 [3072, 768], P('shard'), may hold values from -0.109375 to 0.109375
- outer_bias: bfloat16 [768], P('shard'), may hold values from -1.75 to 1.75
Outputs:
- result: bfloat16 [32, 256, 768], P(('shard', 'rep'))
- input_grad: bfloat16 [32, 256, 768], P(('shard', 'rep'))
- grad_first_gain: float32 [768], P('shard')
- grad_first_shift: float32 [768], P('shard')
- grad_query_weight: float32 [768, 768], P('shard')
- grad_query_bias: float32 [768], P('shard')
- grad_key_weight: float32 [768, 768], P('shard')
- grad_value_weight: float32 [768, 768], P('shard')
- grad_value_bias: float32 [768], P('shard')
- grad_output_weight: float32 [768, 768], P('shard')
- grad_output_bias: float32 [768], P('shard')
- grad_second_gain: float32 [768], P('shard')
- grad_second_shift: float32 [768], P('shard')
- grad_inner_weight: float32 [768, 3072], P('shard')
- grad_inner_bias: float32 [3072], P('shard')
- grad_outer_weight: float32 [3072, 768], P('shard')
- grad_outer_bias: float32 [768], P('shard')
All inputs are finite; a program needn't handle non-finite values.
Results may differ from a plain program's by a relative error of at most 0.019.
Values may be sent and summed in bfloat16 or wider, within the bound.
A program may use at most 128 MiB of HBM per device.

v0:
```python
import functools

import jax
import jax.numpy as jnp
from jax import lax
from jax.experimental import pallas as pl
from jax.experimental.pallas import tpu as pltpu
from jax.sharding import PartitionSpec as P

D = 768
HEADS = 12
HD = 64


EPSILON = 1e-05


def normalize(values, gain, shift):
    center = jnp.mean(values, axis=-1, keepdims=True)
    spread = jnp.mean((values - center) ** 2, axis=-1, keepdims=True)
    inv_std = lax.rsqrt(spread + EPSILON)
    normed = (values - center) * inv_std
    return (normed * gain.astype(jnp.float32) + shift.astype(jnp.float32), normed, inv_std)


def norm_back(grad_out, normed, inv_std, gain):
    scaled = grad_out * gain.astype(jnp.float32)
    return inv_std * (
        scaled
        - jnp.mean(scaled, axis=-1, keepdims=True)
        - normed * jnp.mean(scaled * normed, axis=-1, keepdims=True)
    )


def gelu_parts(inner):
    cdf = 0.5 * (1.0 + jax.scipy.special.erf(inner * 0.7071067811865476))
    density = jnp.exp(-0.5 * inner * inner) * 0.3989422804014327
    return (inner * cdf, cdf + inner * density)


def heads_of(matrix):
    return matrix.reshape(matrix.shape[0], HEADS, HD)


def matmul(left, right):
    return jnp.dot(left, right, preferred_element_type=jnp.float32)


def forward_clip(clip, params):
    (
        first_gain,
        first_shift,
        query_weight,
        query_bias,
        key_weight,
        value_weight,
        value_bias,
        output_weight,
        output_bias,
        second_gain,
        second_shift,
        inner_weight,
        inner_bias,
        outer_weight,
        outer_bias,
    ) = params
    start = clip.astype(jnp.float32)
    normed_one, hat_one, inv_one = normalize(start, first_gain, first_shift)
    first_low = normed_one.astype(jnp.bfloat16)
    query = (
        (matmul(first_low, query_weight) + query_bias.astype(jnp.float32)) * HD ** (-0.5)
    ).astype(jnp.bfloat16)
    keys = matmul(first_low, key_weight).astype(jnp.bfloat16)
    values = (matmul(first_low, value_weight) + value_bias.astype(jnp.float32)).astype(jnp.bfloat16)
    scores = jnp.einsum(
        "qhd,khd->hqk", heads_of(query), heads_of(keys), preferred_element_type=jnp.float32
    )
    highest = jnp.max(scores, axis=-1, keepdims=True)
    log_total = highest + jnp.log(jnp.sum(jnp.exp(scores - highest), axis=-1, keepdims=True))
    probs = jnp.exp(scores - log_total).astype(jnp.bfloat16)
    context = (
        jnp.einsum("hqk,khd->qhd", probs, heads_of(values), preferred_element_type=jnp.float32)
        .reshape(-1, D)
        .astype(jnp.bfloat16)
    )
    mixed = start + matmul(context, output_weight) + output_bias.astype(jnp.float32)
    normed_two, hat_two, inv_two = normalize(mixed, second_gain, second_shift)
    second_low = normed_two.astype(jnp.bfloat16)
    inner = matmul(second_low, inner_weight) + inner_bias.astype(jnp.float32)
    active, slope = gelu_parts(inner)
    active_low = active.astype(jnp.bfloat16)
    result = (mixed + matmul(active_low, outer_weight) + outer_bias.astype(jnp.float32)).astype(
        jnp.bfloat16
    )
    saved = (
        hat_one,
        inv_one,
        first_low,
        query,
        keys,
        values,
        log_total,
        context,
        hat_two,
        inv_two,
        second_low,
        slope,
        active_low,
    )
    return (result, saved)


def backward_clip(grad_low, saved, params):
    (
        first_gain,
        first_shift,
        query_weight,
        query_bias,
        key_weight,
        value_weight,
        value_bias,
        output_weight,
        output_bias,
        second_gain,
        second_shift,
        inner_weight,
        inner_bias,
        outer_weight,
        outer_bias,
    ) = params
    (
        hat_one,
        inv_one,
        first_low,
        query,
        keys,
        values,
        log_total,
        context,
        hat_two,
        inv_two,
        second_low,
        slope,
        active_low,
    ) = saved
    grad = grad_low.astype(jnp.float32)
    g_outer_bias = jnp.sum(grad, axis=0)
    g_outer = matmul(active_low.T, grad_low)
    d_inner = matmul(grad_low, outer_weight.T) * slope
    d_inner_low = d_inner.astype(jnp.bfloat16)
    g_inner_bias = jnp.sum(d_inner, axis=0)
    g_inner = matmul(second_low.T, d_inner_low)
    d_second = matmul(d_inner_low, inner_weight.T)
    g_second_gain = jnp.sum(d_second * hat_two, axis=0)
    g_second_shift = jnp.sum(d_second, axis=0)
    d_mixed = grad + norm_back(d_second, hat_two, inv_two, second_gain)
    d_mixed_low = d_mixed.astype(jnp.bfloat16)
    g_output_bias = jnp.sum(d_mixed, axis=0)
    g_output = matmul(context.T, d_mixed_low)
    d_context = matmul(d_mixed_low, output_weight.T).astype(jnp.bfloat16)
    query_heads = heads_of(query)
    keys_heads = heads_of(keys)
    values_heads = heads_of(values)
    dctx_heads = heads_of(d_context)
    scores = jnp.einsum("qhd,khd->hqk", query_heads, keys_heads, preferred_element_type=jnp.float32)
    probs = jnp.exp(scores - log_total)
    probs_low = probs.astype(jnp.bfloat16)
    d_probs = jnp.einsum(
        "qhd,khd->hqk", dctx_heads, values_heads, preferred_element_type=jnp.float32
    )
    delta = jnp.sum(dctx_heads.astype(jnp.float32) * heads_of(context).astype(jnp.float32), axis=-1)
    d_scores = (probs * (d_probs - jnp.transpose(delta)[:, :, None])).astype(jnp.bfloat16)
    d_values = jnp.einsum(
        "hqk,qhd->khd", probs_low, dctx_heads, preferred_element_type=jnp.float32
    ).reshape(-1, D)
    d_query = jnp.einsum(
        "hqk,khd->qhd", d_scores, keys_heads, preferred_element_type=jnp.float32
    ).reshape(-1, D) * HD ** (-0.5)
    d_keys = jnp.einsum(
        "hqk,qhd->khd", d_scores, query_heads, preferred_element_type=jnp.float32
    ).reshape(-1, D)
    dq_low = d_query.astype(jnp.bfloat16)
    dk_low = d_keys.astype(jnp.bfloat16)
    dv_low = d_values.astype(jnp.bfloat16)
    g_query_bias = jnp.sum(d_query, axis=0)
    g_value_bias = jnp.sum(d_values, axis=0)
    g_query = matmul(first_low.T, dq_low)
    g_keys = matmul(first_low.T, dk_low)
    g_values = matmul(first_low.T, dv_low)
    d_first = (
        matmul(dq_low, query_weight.T)
        + matmul(dk_low, key_weight.T)
        + matmul(dv_low, value_weight.T)
    )
    g_first_gain = jnp.sum(d_first * hat_one, axis=0)
    g_first_shift = jnp.sum(d_first, axis=0)
    d_start = (d_mixed + norm_back(d_first, hat_one, inv_one, first_gain)).astype(jnp.bfloat16)
    grads = (
        g_first_gain,
        g_first_shift,
        g_query,
        g_query_bias,
        g_keys,
        g_values,
        g_value_bias,
        g_output,
        g_output_bias,
        g_second_gain,
        g_second_shift,
        g_inner,
        g_inner_bias,
        g_outer,
        g_outer_bias,
    )
    return (d_start, grads)


MESH = pl.DeviceIdType.MESH


class Ring:
    def __init__(self, chips):
        self.chips = chips
        shard = lax.axis_index("shard")
        self.rep = lax.axis_index("rep")
        self.core = lax.rem(shard, 2)
        chip = shard // 2
        half = chip // 2
        self.pos = half + lax.rem(chip, 2) * (chips - 1 - 2 * half)
        self.step = 1 - 2 * self.core
        self.me = shard
        self.mate = chip * 2 + (1 - self.core)

    def shard_at(self, offset, core):
        place = lax.rem(self.pos + offset + 2 * self.chips, self.chips)
        far = place // (self.chips // 2)
        chip = (1 - far) * 2 * place + far * (2 * (self.chips - 1 - place) + 1)
        return chip * 2 + core

    def next(self):
        return self.shard_at(self.step, self.core)

    def previous(self):
        return self.shard_at(-self.step, self.core)


def rows_of(owner, rows):
    return pl.ds(pl.multiple_of(owner * rows, rows), rows)


def greet(ring, others, reps):
    barrier = pltpu.get_barrier_semaphore()
    for other in others:
        pl.semaphore_signal(barrier, inc=1, device_id=(other, ring.rep), device_id_type=MESH)
    for shift in range(1, reps):
        pl.semaphore_signal(
            barrier,
            inc=1,
            device_id=(ring.me, lax.rem(ring.rep + shift, reps)),
            device_id_type=MESH,
        )
    pl.semaphore_wait(barrier, len(others) + reps - 1)


def gather_kernel(chips, count, *refs):
    ins, outs = refs[:count], refs[count : 2 * count]
    ring_send, ring_recv, mate_send, mate_recv, own_sem = refs[2 * count :]
    ring = Ring(chips)
    core = ring.core
    following, mate = ring.next(), ring.mate
    greet(ring, (following, ring.previous(), mate), 1)

    def where(index, owner):
        return outs[index].at[rows_of(owner, ins[index].shape[0])]

    def to_next(index, step, owner, source):
        return pltpu.make_async_remote_copy(
            src_ref=source,
            dst_ref=where(index, owner),
            send_sem=ring_send.at[step, index],
            recv_sem=ring_recv.at[step, index],
            device_id=(following, ring.rep),
            device_id_type=MESH,
        )

    def to_mate(index, step, owner, source):
        return pltpu.make_async_remote_copy(
            src_ref=source,
            dst_ref=where(index, owner),
            send_sem=mate_send.at[step, index],
            recv_sem=mate_recv.at[step, index],
            device_id=(mate, ring.rep),
            device_id_type=MESH,
        )

    for index in range(count):
        to_next(index, 0, ring.me, ins[index]).start()
    for index in range(count):
        to_mate(index, 0, ring.me, ins[index]).start()
        pltpu.make_async_copy(ins[index], where(index, ring.me), own_sem.at[index]).start()

    def hop(step, carry):
        owner = ring.shard_at(-ring.step * step, core)
        for index in range(count):
            block = where(index, owner)
            to_next(index, step - 1, owner, block).wait_recv()
            pl.when(step < chips - 1)(lambda: to_next(index, step, owner, block).start())
            to_mate(index, step, owner, block).start()
        return carry

    lax.fori_loop(1, chips, hop, 0)

    def finish(step, carry):
        owner = ring.shard_at(-ring.step * step, core)
        theirs = ring.shard_at(ring.step * step, 1 - core)
        for index in range(count):
            to_mate(index, step, theirs, where(index, theirs)).wait_recv()
            to_mate(index, step, owner, where(index, owner)).wait_send()
            pl.when(step < chips - 1)(
                lambda: to_next(index, step, owner, where(index, owner)).wait_send()
            )
        return carry

    lax.fori_loop(0, chips, finish, 0)
    for index in range(count):
        pltpu.make_async_copy(ins[index], where(index, ring.me), own_sem.at[index]).wait()


def gather_all(pieces, shards):
    chips, count = shards // 2, len(pieces)
    return pl.pallas_call(
        functools.partial(gather_kernel, chips, count),
        out_shape=[
            jax.ShapeDtypeStruct((piece.shape[0] * shards, piece.shape[1]), piece.dtype)
            for piece in pieces
        ],
        in_specs=[pl.BlockSpec(memory_space=pltpu.VMEM)] * count,
        out_specs=[pl.BlockSpec(memory_space=pl.ANY)] * count,
        scratch_shapes=[
            pltpu.SemaphoreType.DMA((chips, count)),
            pltpu.SemaphoreType.DMA((chips, count)),
            pltpu.SemaphoreType.DMA((chips, count)),
            pltpu.SemaphoreType.DMA((chips, count)),
            pltpu.SemaphoreType.DMA((count,)),
        ],
        compiler_params=pltpu.CompilerParams(collective_id=0, has_side_effects=True),
        name="gather_all",
    )(*pieces)


def scatter_kernel(chips, reps, count, *refs):
    ins, outs = refs[:count], refs[count : 2 * count]
    held = refs[2 * count : 3 * count]
    arrived = refs[3 * count : 4 * count]
    peers = refs[4 * count : 5 * count]
    ring_send, ring_recv, mate_send, mate_recv, rep_send, rep_recv = refs[5 * count :]
    ring = Ring(chips)
    core = ring.core
    following, mate = ring.next(), ring.mate
    greet(ring, (following, ring.previous(), mate), reps)

    def to_mate(index, step):
        owner = ring.shard_at(ring.step * (step + 1), 1 - core)
        rows = outs[index].shape[0]
        return pltpu.make_async_remote_copy(
            src_ref=ins[index].at[rows_of(owner, rows)],
            dst_ref=held[index].at[step],
            send_sem=mate_send.at[step, index],
            recv_sem=mate_recv.at[step, index],
            device_id=(mate, ring.rep),
            device_id_type=MESH,
        )

    def to_next(index, step):
        return pltpu.make_async_remote_copy(
            src_ref=held[index].at[step],
            dst_ref=arrived[index].at[step],
            send_sem=ring_send.at[step, index],
            recv_sem=ring_recv.at[step, index],
            device_id=(following, ring.rep),
            device_id_type=MESH,
        )

    def to_rep(index, shift):
        return pltpu.make_async_remote_copy(
            src_ref=held[index].at[chips - 1],
            dst_ref=peers[index].at[ring.rep],
            send_sem=rep_send.at[shift, index],
            recv_sem=rep_recv.at[shift, index],
            device_id=(ring.me, lax.rem(ring.rep + shift, reps)),
            device_id_type=MESH,
        )

    def hand_over(step, carry):
        for index in range(count):
            to_mate(index, step).start()
        return carry

    lax.fori_loop(0, chips, hand_over, 0)

    def add(index, step, first):
        owner = ring.shard_at(-ring.step * (step + 1), core)
        rows = outs[index].shape[0]
        to_mate(index, step).wait_recv()
        total = ins[index][rows_of(owner, rows), :].astype(jnp.float32) + held[index][step].astype(
            jnp.float32
        )
        if not first:
            to_next(index, step - 1).wait_recv()
            total = total + arrived[index][step - 1].astype(jnp.float32)
        held[index][step] = total.astype(jnp.bfloat16)

    for index in range(count):
        add(index, 0, True)
        to_next(index, 0).start()

    def hop(step, carry):
        for index in range(count):
            add(index, step, False)
            to_next(index, step).start()
        return carry

    lax.fori_loop(1, chips - 1, hop, 0)
    for index in range(count):
        add(index, chips - 1, False)
        for shift in range(1, reps):
            to_rep(index, shift).start()
        peers[index][ring.rep] = held[index][chips - 1]
    for index in range(count):
        for shift in range(1, reps):
            to_rep(index, shift).wait_recv()
        total = peers[index][0].astype(jnp.float32)
        for rep in range(1, reps):
            total = total + peers[index][rep].astype(jnp.float32)
        outs[index][...] = total

    def finish(step, carry):
        for index in range(count):
            to_mate(index, step).wait_send()
            pl.when(step < chips - 1)(lambda: to_next(index, step).wait_send())
        return carry

    lax.fori_loop(0, chips, finish, 0)
    for index in range(count):
        for shift in range(1, reps):
            to_rep(index, shift).wait_send()


def scatter_all(pieces, shards, reps):
    chips, count = shards // 2, len(pieces)
    blocks = [(piece.shape[0] // shards, piece.shape[1]) for piece in pieces]
    return pl.pallas_call(
        functools.partial(scatter_kernel, chips, reps, count),
        out_shape=[jax.ShapeDtypeStruct(block, jnp.float32) for block in blocks],
        in_specs=[pl.BlockSpec(memory_space=pltpu.VMEM)] * count,
        out_specs=[pl.BlockSpec(memory_space=pltpu.VMEM)] * count,
        scratch_shapes=[pltpu.VMEM((chips,) + block, jnp.bfloat16) for block in blocks]
        + [pltpu.VMEM((chips - 1,) + block, jnp.bfloat16) for block in blocks]
        + [pltpu.VMEM((reps,) + block, jnp.bfloat16) for block in blocks]
        + [pltpu.SemaphoreType.DMA((chips, count))] * 4
        + [pltpu.SemaphoreType.DMA((reps, count))] * 2,
        compiler_params=pltpu.CompilerParams(
            collective_id=1, has_side_effects=True, vmem_limit_bytes=60 * 1024 * 1024
        ),
        name="scatter_all",
    )(*pieces)


NARROW = (0, 1, 3, 6, 8, 9, 10, 14)
WIDE = 12
WEIGHTS = (2, 4, 5, 7, 11, 13)
LANES = 128
SUBLANES = 16


def packed_rows(size):
    return -(-size // (LANES * SUBLANES)) * SUBLANES


def pack(vectors, owners):
    flat = jnp.concatenate(
        [vectors[i].reshape(owners, -1) for i in NARROW] + [vectors[WIDE].reshape(owners, -1)],
        axis=1,
    )
    rows = packed_rows(flat.shape[1])
    flat = jnp.pad(flat, ((0, 0), (0, rows * LANES - flat.shape[1])))
    return flat.reshape(owners * rows, LANES)


def unpack(block, owners, narrow, wide):
    flat = block.reshape(owners, -1)
    count = len(NARROW)
    first = flat[:, : count * narrow].reshape(owners, count, narrow)
    first = jnp.transpose(first, (1, 0, 2)).reshape(count, owners * narrow)
    found = {i: first[k] for k, i in enumerate(NARROW)}
    found[WIDE] = flat[:, count * narrow : count * narrow + wide].reshape(-1)
    return found


def per_device(shards, reps, frames, cotangent, *local):
    narrow, wide = local[0].shape[0], local[WIDE].shape[0]
    gathered = gather_all([local[i] for i in WEIGHTS] + [pack(local, 1)], shards)
    params = [None] * len(local)
    for k, i in enumerate(WEIGHTS):
        params[i] = gathered[k]
    for i, vector in unpack(gathered[-1], shards, narrow, wide).items():
        params[i] = vector
    params = tuple(params)

    results, input_grads, totals = [], [], None
    for k in range(frames.shape[0]):
        result, saved = forward_clip(frames[k], params)
        d_start, grads = backward_clip(cotangent[k], saved, params)
        results.append(result)
        input_grads.append(d_start)
        totals = grads if totals is None else tuple(a + b for a, b in zip(totals, grads))

    low = [total.astype(jnp.bfloat16) for total in totals]
    summed = scatter_all([low[i] for i in WEIGHTS] + [pack(low, shards)], shards, reps)
    out = [None] * len(local)
    for k, i in enumerate(WEIGHTS):
        out[i] = summed[k]
    for i, vector in unpack(summed[-1], 1, narrow, wide).items():
        out[i] = vector
    return (jnp.stack(results), jnp.stack(input_grads), *out)


def solution(mesh):
    clips = P(("shard", "rep"), None, None)
    weights = tuple(P("shard", None) if i in WEIGHTS else P("shard") for i in range(15))
    return jax.shard_map(
        functools.partial(per_device, mesh.shape["shard"], mesh.shape["rep"]),
        mesh=mesh,
        in_specs=(clips, clips) + weights,
        out_specs=(clips, clips) + weights,
        check_vma=False,
    )
```

profile of v0, /device:TPU:0, one launch (start us, length us, event | category | flops | bytes accessed | tf_op | source)
XLA Modules:
  0.0 263.3 jit_solution(4524231856505404835)
XLA Ops:
  0.7 0.7 reshape.376
  1.3 1.2 convert_reduce_fusion
  2.5 1.2 fusion.28
  3.8 0.9 concatenate.6
  4.7 0.6 pad_reduce_fusion
  5.3 1.1 reduce_sum.191
  6.4 0.7 reshape.384
  7.0 77.6 %gather_all.1 = (bf16[768,768]{1,0:T(8,128)(2,1)}, bf16[768,768]{1,0:T(8,128)(2,1)}, bf16[768,768]{1,0:T(8,128)(2,1)}, bf16[768,768]{1,0:T(8,128)(2,1)}, bf16[76...) custom-call(bf16[48,768]{1,0:T(8,128)(2,1)} %refs_0_.1, bf16[48,768]{1,0:T(8,128)(2,1)} %refs_1_.1, ...), custom_call_target="tpu_custom_call" | custom-call | tf_op jit(solution)/shard_map/gather_all/pallas_call | solution.py:331
  84.7 1.0 reshape.378
  85.7 0.7 reshape.395
  86.7 0.7 reshape.396
  87.5 0.7 reshape.393
  88.1 0.7 reshape.394
  88.8 0.7 reshape.392
  89.6 2.0 fusion.10
  91.7 0.9 copy.46
  93.2 0.9 copy.47
  94.7 0.9 copy.48
  95.6 1.9 fusion.60
  98.0 0.6 convolution_convert_fusion.8
  98.7 0.8 copy-done.5
  99.4 0.6 fusion.61
  100.3 3.7 %multiply_convert_fusion.1 = (bf16[256,3072]{1,0:T(8,128)(2,1)S(1)}, f32[256,3072]{1,0:T(8,128)S(1)}) fusion(f32[3072]{0:T(1024)S(1)} %copy-done.41, bf16[768,3072]{1,0:T(8,128)(2,1)} %get-tuple-element.36, f32[256,768]{1,0:T(8,128)S(1)} %get-tuple-element.78, f32[768]{0:T(1024)S(1)} %copy-done.29, f32[768]{0:T(1024)S(1)} %copy-done.27, ...), kind=kOutput, calls=%fused_computation.11 | convolution fusion | flops 1213661184 | bytes 10244096 | tf_op jit(solution)/shard_map/dot_general | solution.py:46
  104.2 2.9 %fusion.62 = (bf16[3072]{0:T(1024)(128)(2,1)}, bf16[256,3072]{1,0:T(8,128)(2,1)S(1)}) fusion(f32[256,3072]{1,0:T(8,128)S(1)} %get-tuple-element.80, bf16[3072,768]{1,0:T(8,128)(2,1)S(1)} %bitcast.181, bf16[1,256,768]{2,1,0:T(8,128)(2,1)S(1)} %copy-done.10), kind=kOutput, calls=%fused_computation.121 | convolution fusion | flops 1216607232 | bytes 9836544 | tf_op jit(solution)/shard_map/dot_general | solution.py:46
  107.1 2.2 fusion.12
  109.3 3.1 %multiply_reduce_fusion = (bf16[768]{0:T(1024)(128)(2,1)}, f32[256]{0:T(256)}, f32[256]{0:T(256)}, bf16[768]{0:T(1024)(128)(2,1)}, f32[256,768]{1,0:T(8,128)}) fusion(f32[256,768]{1,0:T(8,128)S(1)} %get-tuple-element.78, f32[256]{0:T(256)S(1)} %add_rsqrt_fusion, f32[256]{0:T(256)S(1)} %broadcast_multiply_fusion.4, f32[768]{0:T(1024)S(1)} %copy-done.27, ...), kind=kOutput, calls=%fused_computation.64 | convolution fusion | flops 1209726976 | bytes 7874560 | tf_op jit(solution)/shard_map/dot_general | solution.py:46
  112.4 1.4 convert_element_type.348
  113.8 1.4 convert_element_type.352
  115.2 0.8 broadcast_multiply_fusion.2
  115.9 2.4 fusion.58
  118.4 0.9 copy-done.2
  119.2 1.3 convolution_convert_fusion.7
  120.5 1.9 copy.50
  122.4 1.4 convert_element_type.346
  123.8 1.4 convert_element_type.350
  125.1 1.3 multiply_reduce_fusion.1
  126.5 2.3 fusion.59
  128.8 0.8 multiply_convert_fusion
  129.9 0.6 convolution_convert_fusion.6
  130.5 1.2 bitcast_convert_fusion
  133.0 1.4 fusion.27
  134.4 0.7 convert_element_type.344
  135.1 0.7 broadcast_multiply_fusion
  135.7 0.7 broadcast_multiply_fusion.1
  136.4 1.7 fusion.39
  138.2 1.5 convolution_convert_fusion.2.refs_3_
  139.6 0.8 convert_element_type.338
  140.5 0.8 convert_element_type.340
  141.5 0.8 concatenate.7
  142.3 0.7 reshape.385.refs_6_
  143.0 2.5 convolution_convert_fusion.3.refs_2_
  145.6 2.4 convolution_convert_fusion.4.refs_1_
  147.9 2.4 convolution_convert_fusion.5.refs_0_
  150.4 3.7 %convolution_convert_fusion.1.refs_4_ = bf16[768,3072]{1,0:T(8,128)(2,1)} fusion(bf16[256,3072]{1,0:T(8,128)(2,1)S(1)} %copy-done.19, f32[256,768]{1,0:T(8,128)S(1)} %copy-done.1, f32[768]{0:T(1024)S(1)} %copy-done.30, f32[768]{0:T(1024)S(1)} %copy-done.28, f32[256]{0:T(256)S(1)} %copy-done.40, f32[256]{0:T(256)S(1)} %copy-done.33), kind=kOutput, calls=%fused_computation.1 | convolution fusion | flops 1211301888 | bytes 7086080 | tf_op jit(solution)/shard_map/dot_general | solution.py:46
  154.1 3.8 %convolution_convert_fusion.refs_5_ = bf16[3072,768]{1,0:T(8,128)(2,1)} fusion(bf16[256,3072]{1,0:T(8,128)(2,1)S(1)} %copy-done.13, bf16[1,256,768]{2,1,0:T(8,128)(2,1)S(1)} %copy-done.11), kind=kOutput, calls=%fused_computation | convolution fusion | flops 1210318848 | bytes 6684672 | tf_op jit(solution)/shard_map/dot_general | solution.py:46
  158.0 92.5 %scatter_all.1 = (f32[48,768]{1,0:T(8,128)}, f32[48,768]{1,0:T(8,128)}, f32[48,768]{1,0:T(8,128)}, f32[48,768]{1,0:T(8,128)}, f32[48,3072]{1,0:T(8,128)}, /*index=5*/f32[192,768]{1,0:T(8,128)}, f32[16,128]{1,0:T(8,128)}) custom-call(bf16[768,768]{1,0:T(8,128)(2,1)} %convolution_convert_fusion.5.refs_0_, bf16[768,768]{1,0:T(8,128)(2,1)} %convolution_convert_fusion.4.refs_1_, ...), custom_call_target="tpu_custom_call" | custom-call | tf_op jit(solution)/shard_map/scatter_all/pallas_call | solution.py:452
  250.4 1.2 slice.118
  251.7 1.4 slice_bitcast_fusion
  253.1 1.6 copy.66
  254.7 1.6 copy.67
  256.3 1.6 copy.68
  257.8 1.6 copy.69
  259.4 1.9 copy.70
  261.3 1.9 copy.71
  (128 shorter events, 4.4 us)
Async XLA Ops:
  1.3 91.3 %copy-start.4 = (bf16[1,256,768]{2,1,0:T(8,128)(2,1)S(1)}, bf16[1,256,768]{2,1,0:T(8,128)(2,1)}, u32[]{:S(2)}) copy-start(bf16[1,256,768]{2,1,0:T(8,128)(2,1)} %param.17) | copy-start | bytes 1179652
  2.5 91.6 %copy-start.42 = (f32[256]{0:T(256)}, f32[256]{0:T(256)S(1)}, u32[]{:S(2)}) copy-start(f32[256]{0:T(256)S(1)} %broadcast_multiply_fusion.5) | copy-start | bytes 3076
  3.8 90.3 %copy-start.44 = (f32[256]{0:T(256)}, f32[256]{0:T(256)S(1)}, u32[]{:S(2)}) copy-start(f32[256]{0:T(256)S(1)} %add_rsqrt_fusion.1) | copy-start | bytes 3076
  84.7 7.9 %copy-start.22 = (bf16[768,768]{1,0:T(8,128)(2,1)S(1)}, bf16[768,768]{1,0:T(8,128)(2,1)}, u32[]{:S(2)}) copy-start(bf16[768,768]{1,0:T(8,128)(2,1)} %get-tuple-element.33) | copy-start | bytes 3538948
  87.4 6.7 %copy-start.34 = (f32[768]{0:T(1024)}, f32[768]{0:T(1024)S(1)}, u32[]{:S(2)}) copy-start(f32[768]{0:T(1024)S(1)} %reshape.388) | copy-start | bytes 9220
  87.5 6.6 %copy-start.46 = (f32[768]{0:T(1024)}, f32[768]{0:T(1024)S(1)}, u32[]{:S(2)}) copy-start(f32[768]{0:T(1024)S(1)} %reshape.389) | copy-start | bytes 9220
  89.6 4.5 %copy-start.20 = (bf16[768,768]{1,0:T(8,128)(2,1)S(1)}, bf16[768,768]{1,0:T(8,128)(2,1)}, u32[]{:S(2)}) copy-start(bf16[768,768]{1,0:T(8,128)(2,1)} %get-tuple-element.34) | copy-start | bytes 3538948
  95.6 2.4 copy-start.16
  95.6 8.5 %slice-start.2 = ((s8[4718592]{0:T(1024)(128)(4,1)}), s8[4194304]{0:T(1024)(128)(4,1)S(1)}, s32[]{:S(2)}) async-start(s8[4718592]{0:T(1024)(128)(4,1)} %bitcast.180), calls=%async_computation.2 | async-start | bytes 8388608
  97.5 1.9 copy-start.8
  97.5 1.9 copy-start.36
  98.0 2.3 copy-start.27
  98.0 2.3 copy-start.29
  98.0 2.3 copy-start.41
  98.6 0.8 copy-start.5
  99.4 4.7 %slice-start.3 = ((s8[4718592]{0:T(1024)(128)(4,1)}), s8[524288]{0:T(1024)(128)(4,1)S(1)}, s32[]{:S(2)}) async-start(s8[4718592]{0:T(1024)(128)(4,1)} %bitcast.180), calls=%async_computation.3 | async-start | bytes 1048576
  100.0 9.3 %copy-start = (f32[256,768]{1,0:T(8,128)}, f32[256,768]{1,0:T(8,128)S(1)}, u32[]{:S(2)}) copy-start(f32[256,768]{1,0:T(8,128)S(1)} %get-tuple-element.78) | copy-start | bytes 2359300
  100.0 9.3 %copy-start.32 = (f32[256]{0:T(256)}, f32[256]{0:T(256)S(1)}, u32[]{:S(2)}) copy-start(f32[256]{0:T(256)S(1)} %broadcast_multiply_fusion.4) | copy-start | bytes 3076
  100.3 9.0 %copy-start.39 = (f32[256]{0:T(256)}, f32[256]{0:T(256)S(1)}, u32[]{:S(2)}) copy-start(f32[256]{0:T(256)S(1)} %add_rsqrt_fusion) | copy-start | bytes 3076
  100.3 3.8 %copy-start.10 = (bf16[1,256,768]{2,1,0:T(8,128)(2,1)S(1)}, bf16[1,256,768]{2,1,0:T(8,128)(2,1)}, u32[]{:S(2)}) copy-start(bf16[1,256,768]{2,1,0:T(8,128)(2,1)} %param.18) | copy-start | bytes 1179652
  100.3 9.0 %slice-start = ((s8[4718592]{0:T(1024)(128)(4,1)}), s8[4194304]{0:T(1024)(128)(4,1)S(1)}, s32[]{:S(2)}) async-start(s8[4718592]{0:T(1024)(128)(4,1)} %bitcast.178), calls=%async_computation | async-start | bytes 8388608
  104.1 3.0 %copy-start.12 = (bf16[256,3072]{1,0:T(8,128)(2,1)}, bf16[256,3072]{1,0:T(8,128)(2,1)S(1)}, u32[]{:S(2)}) copy-start(bf16[256,3072]{1,0:T(8,128)(2,1)S(1)} %get-tuple-element.79) | copy-start | bytes 4718596
  104.1 3.0 %copy-start.47 = (f32[768]{0:T(1024)S(1)}, f32[768]{0:T(1024)}, u32[]{:S(2)}) copy-start(f32[768]{0:T(1024)} %reshape.396) | copy-start | bytes 9220
  104.2 5.2 %slice-start.1 = ((s8[4718592]{0:T(1024)(128)(4,1)}), s8[524288]{0:T(1024)(128)(4,1)S(1)}, s32[]{:S(2)}) async-start(s8[4718592]{0:T(1024)(128)(4,1)} %bitcast.178), calls=%async_computation.1 | async-start | bytes 1048576
  107.1 2.2 copy-start.18
  115.2 4.1 %copy-start.9 = (bf16[768,768]{1,0:T(8,128)(2,1)S(1)}, bf16[768,768]{1,0:T(8,128)(2,1)}, u32[]{:S(2)}) copy-start(bf16[768,768]{1,0:T(8,128)(2,1)} %get-tuple-element.35) | copy-start | bytes 3538948
  118.4 0.9 copy-start.2
  125.1 3.6 %copy-start.7 = (bf16[256,768]{0,1:T(8,128)(2,1)S(1)}, bf16[256,768]{0,1:T(8,128)(2,1)}, u32[]{:S(2)}) copy-start(bf16[256,768]{0,1:T(8,128)(2,1)} %copy.50) | copy-start | bytes 1179652
  125.1 3.6 %copy-start.17 = (bf16[256,768]{0,1:T(8,128)(2,1)S(1)}, bf16[256,768]{0,1:T(8,128)(2,1)}, u32[]{:S(2)}) copy-start(bf16[256,768]{0,1:T(8,128)(2,1)} %copy.46) | copy-start | bytes 1179652
  128.8 4.0 %copy-start.24 = (bf16[256,12,64]{0,2,1:T(8,128)(2,1)}, bf16[256,12,64]{0,2,1:T(8,128)(2,1)S(1)}, u32[]{:S(2)}) copy-start(bf16[256,12,64]{0,2,1:T(8,128)(2,1)S(1)} %get-tuple-element.64) | copy-start | bytes 1179652
  128.8 1.1 copy-start.15
  128.8 1.7 copy-start.14
  129.9 1.8 copy-start.23
  130.5 1.7 copy-start.21
  131.7 1.1 copy-start.35
  131.7 1.1 copy-start.43
  131.7 1.1 copy-start.45
  131.7 1.3 copy-start.48
  132.2 2.2 copy-start.37
  132.2 4.2 %copy-start.3 = (f32[256,768]{1,0:T(8,128)S(1)}, f32[256,768]{1,0:T(8,128)}, u32[]{:S(2)}) copy-start(f32[256,768]{1,0:T(8,128)} %copy-done.2) | copy-start | bytes 2359300
  132.8 5.4 %copy-start.6 = (bf16[12,64,256]{2,1,0:T(8,128)(2,1)S(1)}, bf16[12,64,256]{2,1,0:T(8,128)(2,1)}, u32[]{:S(2)}) copy-start(bf16[12,64,256]{2,1,0:T(8,128)(2,1)} %copy-done.5) | copy-start | bytes 1179652
  134.4 7.1 %copy-start.31 = (bf16[16,192]{1,0:T(8,128)(2,1)S(1)}, bf16[16,192]{1,0:T(8,128)(2,1)}, u32[]{:S(2)}) copy-start(bf16[16,192]{1,0:T(8,128)(2,1)} %convert_element_type.352) | copy-start | bytes 18436
  135.1 6.5 %copy-start.38 = (bf16[16,48]{1,0:T(8,128)(2,1)S(1)}, bf16[16,48]{1,0:T(8,128)(2,1)}, u32[]{:S(2)}) copy-start(bf16[16,48]{1,0:T(8,128)(2,1)} %reshape.384) | copy-start | bytes 4612
  138.2 4.8 %copy-start.25 = (bf16[256,12,64]{0,2,1:T(8,128)(2,1)S(1)}, bf16[256,12,64]{0,2,1:T(8,128)(2,1)}, u32[]{:S(2)}) copy-start(bf16[256,12,64]{0,2,1:T(8,128)(2,1)} %copy-done.24) | copy-start | bytes 1179652
  139.6 8.3 %copy-start.26 = (bf16[256,12,64]{0,2,1:T(8,128)(2,1)S(1)}, bf16[256,12,64]{0,2,1:T(8,128)(2,1)}, u32[]{:S(2)}) copy-start(bf16[256,12,64]{0,2,1:T(8,128)(2,1)} %get-tuple-element.65) | copy-start | bytes 1179652
  143.0 7.4 %copy-start.1 = (f32[256,768]{1,0:T(8,128)S(1)}, f32[256,768]{1,0:T(8,128)}, u32[]{:S(2)}) copy-start(f32[256,768]{1,0:T(8,128)} %copy-done) | copy-start | bytes 2359300
  143.0 7.4 %copy-start.19 = (bf16[256,3072]{1,0:T(8,128)(2,1)S(1)}, bf16[256,3072]{1,0:T(8,128)(2,1)}, u32[]{:S(2)}) copy-start(bf16[256,3072]{1,0:T(8,128)(2,1)} %copy-done.18) | copy-start | bytes 4718596
  143.0 7.4 %copy-start.28 = (f32[768]{0:T(1024)S(1)}, f32[768]{0:T(1024)}, u32[]{:S(2)}) copy-start(f32[768]{0:T(1024)} %reshape.393) | copy-start | bytes 9220
  143.0 7.4 %copy-start.30 = (f32[768]{0:T(1024)S(1)}, f32[768]{0:T(1024)}, u32[]{:S(2)}) copy-start(f32[768]{0:T(1024)} %reshape.394) | copy-start | bytes 9220
  143.0 7.4 %copy-start.33 = (f32[256]{0:T(256)S(1)}, f32[256]{0:T(256)}, u32[]{:S(2)}) copy-start(f32[256]{0:T(256)} %copy-done.32) | copy-start | bytes 3076
  143.0 7.4 %copy-start.40 = (f32[256]{0:T(256)S(1)}, f32[256]{0:T(256)}, u32[]{:S(2)}) copy-start(f32[256]{0:T(256)} %copy-done.39) | copy-start | bytes 3076
  150.4 3.7 %copy-start.11 = (bf16[1,256,768]{2,1,0:T(8,128)(2,1)S(1)}, bf16[1,256,768]{2,1,0:T(8,128)(2,1)}, u32[]{:S(2)}) copy-start(bf16[1,256,768]{2,1,0:T(8,128)(2,1)} %param.18) | copy-start | bytes 1179652
  150.4 3.7 %copy-start.13 = (bf16[256,3072]{1,0:T(8,128)(2,1)S(1)}, bf16[256,3072]{1,0:T(8,128)(2,1)}, u32[]{:S(2)}) copy-start(bf16[256,3072]{1,0:T(8,128)(2,1)} %copy-done.12) | copy-start | bytes 4718596
where the time goes:
time: 264 us; the launch traced here: 263 us
  Pallas kernels  170 us (64%)
  matrix products  43 us (16%)
  local copies, waits for them, and re-layouts  36.6 us (14%)
  other arithmetic  12.2 us (5%)
    pallas_call x1, Pallas kernels, scatter_all(): pl.pallas_call(functools.partial(scatter_kernel, chips, reps, count), out...  92.5 us
    pallas_call x1, Pallas kernels, gather_all(): pl.pallas_call(functools.partial(gather_kernel, chips, count), out_shape=...  77.6 us
    dot_general x18, matrix products, matmul(): return jnp.dot(left, right, preferred_element_type=jnp.float32)  35.7 us
    unnamed x112, local copies, waits for them, and re-layouts  12.5 us
    convert_element_type x8, local copies, waits for them, and re-layouts, per_device(): low = [total.astype(jnp.bfloat16) for total in totals]  7.8 us

commit v1 on v0

--- a/solution.py
+++ b/solution.py
@@ -497,7 +497,7 @@
     return found
 
 
-def per_device(shards, reps, frames, cotangent, *local):
+def per_device_plain(shards, reps, frames, cotangent, *local):
     narrow, wide = local[0].shape[0], local[WIDE].shape[0]
     gathered = gather_all([local[i] for i in WEIGHTS] + [pack(local, 1)], shards)
     params = [None] * len(local)
@@ -523,6 +523,805 @@
     for i, vector in unpack(summed[-1], 1, narrow, wide).items():
         out[i] = vector
     return (jnp.stack(results), jnp.stack(input_grads), *out)
+
+
+TN = (((0,), (0,)), ((), ()))
+NT = (((1,), (1,)), ((), ()))
+CHUNK = 256
+BLOCK = 32
+
+
+def dot_tn(left, right):
+    return lax.dot_general(left, right, TN, preferred_element_type=jnp.float32)
+
+
+def dot_nt(left, right):
+    return lax.dot_general(left, right, NT, preferred_element_type=jnp.float32)
+
+
+def span(start, size, unit):
+    return pl.ds(pl.multiple_of(start, unit), size)
+
+
+class Gather:
+    def __init__(self, ring, chips, ins, outs, crossed, sems):
+        self.ring, self.chips, self.ins, self.outs, self.crossed = ring, chips, ins, outs, crossed
+        (
+            self.ring_send,
+            self.ring_recv,
+            self.mate_send,
+            self.mate_recv,
+            self.peer_send,
+            self.peer_recv,
+            self.own_sem,
+        ) = sems
+        self.next, self.mate = ring.next(), ring.mate
+
+    def rows(self, i):
+        return self.ins[i].shape[0]
+
+    def part(self, i, kind):
+        rows, cross = self.rows(i), self.crossed[i]
+        if kind == "all":
+            return 0, rows
+        if kind == "ringed":
+            return self.ring.rep * cross, rows - cross
+        if kind == "sent":
+            return self.ring.rep * (rows - cross), cross
+        return (1 - self.ring.rep) * (rows - cross), cross
+
+    def remote(self, i, step, owner, kind, send, recv, target, own=False):
+        offset, size = self.part(i, kind)
+        place = self.outs[i].at[span(owner * self.rows(i) + offset, size, SUBLANES)]
+        source = self.ins[i].at[span(offset, size, SUBLANES)] if own else place
+        return pltpu.make_async_remote_copy(
+            src_ref=source,
+            dst_ref=place,
+            send_sem=send.at[step, i],
+            recv_sem=recv.at[step, i],
+            device_id=target,
+            device_id_type=MESH,
+        )
+
+    def to_next(self, i, step, owner, own=False):
+        target = (self.next, self.ring.rep)
+        return self.remote(
+            i, step, owner, "ringed", self.ring_send, self.ring_recv, target, own
+        )
+
+    def to_mate(self, i, step, owner, kind, own=False):
+        target = (self.mate, self.ring.rep)
+        return self.remote(i, step, owner, kind, self.mate_send, self.mate_recv, target, own)
+
+    def to_peer(self, i, step, owner, kind):
+        target = (self.ring.me, 1 - self.ring.rep)
+        return self.remote(i, step, owner, kind, self.peer_send, self.peer_recv, target)
+
+    def own_copy(self, i):
+        place = self.outs[i].at[span(self.ring.me * self.rows(i), self.rows(i), SUBLANES)]
+        return pltpu.make_async_copy(self.ins[i], place, self.own_sem.at[i])
+
+    def owner(self, step):
+        return self.ring.shard_at(-self.ring.step * step, self.ring.core)
+
+    def start(self, i):
+        self.to_next(i, 0, self.ring.me, True).start()
+        self.to_mate(i, 0, self.ring.me, "all", True).start()
+        self.own_copy(i).start()
+
+    def hop(self, i, step):
+        owner = self.owner(step)
+        self.to_next(i, step - 1, owner).wait_recv()
+        if step < self.chips - 1:
+            self.to_next(i, step, owner).start()
+        if self.crossed[i]:
+            self.to_peer(i, step, owner, "sent").start()
+        self.to_mate(i, step, owner, "ringed").start()
+
+    def cross(self, i, step):
+        if self.crossed[i]:
+            owner = self.owner(step)
+            self.to_peer(i, step, owner, "got").wait_recv()
+            self.to_mate(i, step, owner, "got").start()
+
+    def finish(self, i):
+        for step in range(self.chips):
+            theirs = self.ring.shard_at(self.ring.step * step, 1 - self.ring.core)
+            self.to_mate(i, step, theirs, "all").wait_recv()
+        self.own_copy(i).wait()
+
+    def drain(self, i):
+        for step in range(self.chips):
+            owner = self.owner(step)
+            self.to_mate(i, step, owner, "all").wait_send()
+            if step < self.chips - 1:
+                self.to_next(i, step, owner).wait_send()
+            if step and self.crossed[i]:
+                self.to_peer(i, step, owner, "sent").wait_send()
+
+
+class Scatter:
+    def __init__(self, ring, chips, terms, outs, held, arrived, peers, others, crossed, sems):
+        self.ring, self.chips, self.terms, self.outs = ring, chips, terms, outs
+        self.held, self.arrived, self.peers, self.others = held, arrived, peers, others
+        self.crossed = crossed
+        (
+            self.mate_send,
+            self.mate_recv,
+            self.ring_send,
+            self.ring_recv,
+            self.peer_send,
+            self.peer_recv,
+            self.last_send,
+            self.last_recv,
+        ) = sems
+        self.next, self.mate = ring.next(), ring.mate
+
+    def rows(self, i):
+        return self.outs[i].shape[0]
+
+    def spots(self, i):
+        rep, rows, cross = self.ring.rep, self.rows(i), self.crossed[i]
+        return {
+            "ringed": rep * cross,
+            "kept": rep * (rows - cross),
+            "middle": cross,
+            "given": (1 - rep) * (rows - cross),
+            "kept_in": rep * (rows - 2 * cross),
+            "middle_in": (1 - rep) * cross,
+            "other_kept_in": (1 - rep) * (rows - 2 * cross),
+            "other_middle_in": rep * cross,
+        }
+
+    def copy(self, source, target, send, recv, device):
+        return pltpu.make_async_remote_copy(
+            src_ref=source,
+            dst_ref=target,
+            send_sem=send,
+            recv_sem=recv,
+            device_id=device,
+            device_id_type=MESH,
+        )
+
+    def owner(self, step):
+        return self.ring.shard_at(-self.ring.step * (step + 1), self.ring.core)
+
+    def to_mate(self, i, step):
+        owner = self.ring.shard_at(self.ring.step * (step + 1), 1 - self.ring.core)
+        return self.copy(
+            self.terms[i].at[rows_of(owner, self.rows(i))],
+            self.held[i].at[step],
+            self.mate_send.at[step, i],
+            self.mate_recv.at[step, i],
+            (self.mate, self.ring.rep),
+        )
+
+    def to_next(self, i, step):
+        size = self.rows(i) - self.crossed[i]
+        return self.copy(
+            self.held[i].at[step, span(self.spots(i)["ringed"], size, SUBLANES)],
+            self.arrived[i].at[step],
+            self.ring_send.at[step, i],
+            self.ring_recv.at[step, i],
+            (self.next, self.ring.rep),
+        )
+
+    def to_peer(self, i, step):
+        return self.copy(
+            self.held[i].at[step, span(self.spots(i)["given"], self.crossed[i], SUBLANES)],
+            self.peers[i].at[step],
+            self.peer_send.at[step, i],
+            self.peer_recv.at[step, i],
+            (self.ring.me, 1 - self.ring.rep),
+        )
+
+    def to_last(self, i):
+        size = self.rows(i) - self.crossed[i]
+        return self.copy(
+            self.held[i].at[self.chips - 1, span(self.spots(i)["ringed"], size, SUBLANES)],
+            self.others[i],
+            self.last_send.at[i],
+            self.last_recv.at[i],
+            (self.ring.me, 1 - self.ring.rep),
+        )
+
+    def start(self, i):
+        for step in range(self.chips):
+            self.to_mate(i, step).start()
+
+    def both(self, i, step, offset, size):
+        mine = self.terms[i][span(self.owner(step) * self.rows(i) + offset, size, SUBLANES), :]
+        theirs = self.held[i][step, span(offset, size, SUBLANES), :]
+        return mine.astype(jnp.float32) + theirs.astype(jnp.float32)
+
+    def keep(self, i, step, offset, total):
+        place = span(offset, total.shape[0], SUBLANES)
+        self.held[i][step, place, :] = total.astype(jnp.bfloat16)
+
+    def give(self, i, step):
+        self.to_mate(i, step).wait_recv()
+        if self.crossed[i]:
+            offset = self.spots(i)["given"]
+            self.keep(i, step, offset, self.both(i, step, offset, self.crossed[i]))
+            self.to_peer(i, step).start()
+
+    def hop(self, i, step):
+        spots, cross = self.spots(i), self.crossed[i]
+        middle = self.rows(i) - 2 * cross
+        if step:
+            self.to_next(i, step - 1).wait_recv()
+        total = self.both(i, step, spots["middle"], middle)
+        if step:
+            part = self.arrived[i][step - 1, span(spots["middle_in"], middle, SUBLANES), :]
+            total = total + part.astype(jnp.float32)
+        self.keep(i, step, spots["middle"], total)
+        if cross:
+            self.to_peer(i, step).wait_recv()
+            total = self.both(i, step, spots["kept"], cross)
+            total = total + self.peers[i][step].astype(jnp.float32)
+            if step:
+                part = self.arrived[i][step - 1, span(spots["kept_in"], cross, SUBLANES), :]
+                total = total + part.astype(jnp.float32)
+            self.keep(i, step, spots["kept"], total)
+        if step < self.chips - 1:
+            self.to_next(i, step).start()
+        else:
+            self.to_last(i).start()
+
+    def finish(self, i):
+        spots, cross = self.spots(i), self.crossed[i]
+        middle, last = self.rows(i) - 2 * cross, self.chips - 1
+        self.to_last(i).wait_recv()
+        mine = self.held[i][last, span(spots["middle"], middle, SUBLANES), :]
+        theirs = self.others[i][span(spots["other_middle_in"], middle, SUBLANES), :]
+        self.outs[i][span(spots["middle"], middle, SUBLANES), :] = mine.astype(
+            jnp.float32
+        ) + theirs.astype(jnp.float32)
+        if cross:
+            kept = span(spots["kept"], cross, SUBLANES)
+            self.outs[i][kept, :] = self.held[i][last, kept, :].astype(jnp.float32)
+            other = self.others[i][span(spots["other_kept_in"], cross, SUBLANES), :]
+            given = span(spots["given"], cross, SUBLANES)
+            self.outs[i][given, :] = other.astype(jnp.float32)
+
+    def drain(self, i):
+        for step in range(self.chips):
+            self.to_mate(i, step).wait_send()
+            if step < self.chips - 1:
+                self.to_next(i, step).wait_send()
+            if self.crossed[i]:
+                self.to_peer(i, step).wait_send()
+        self.to_last(i).wait_send()
+
+
+Q, K, V, O, INNER, OUTER, PACK = range(7)
+SLOTS = 16
+SPREAD = len(NARROW)
+VECTOR = {name: row for row, name in enumerate(NARROW)}
+
+
+def iota(shape, axis):
+    return lax.broadcasted_iota(jnp.int32, shape, axis)
+
+
+def one_hot(condition):
+    return jnp.where(condition, 1.0, 0.0).astype(jnp.bfloat16)
+
+
+def bits(size):
+    return size.bit_length() - 1
+
+
+def packed_slots(index, shards, ratio):
+    owner, slot = index >> bits(SLOTS), index & (SLOTS - 1)
+    wide = owner * ratio + slot - SPREAD
+    line = jnp.where(slot < SPREAD, slot, SPREAD + (wide >> bits(shards)))
+    group = jnp.where(slot < SPREAD, owner, wide & (shards - 1))
+    return line, group, slot < SPREAD + ratio
+
+
+def pick_table(shards, ratio):
+    shape = (SLOTS, shards * SLOTS)
+    line, _, used = packed_slots(iota(shape, 1), shards, ratio)
+    return one_hot(used & (line == iota(shape, 0)))
+
+
+def group_mask(shards, ratio, narrow, width):
+    shape = (shards * SLOTS, width)
+    _, group, used = packed_slots(iota(shape, 0), shards, ratio)
+    column = iota(shape, 1) - group * narrow
+    return used & (column >= 0) & (column < narrow)
+
+
+def place_table(shards, narrow, width):
+    lane = iota((width, LANES), 1)
+    ahead = iota((width, LANES), 0) - lane
+    found = ahead == 0
+    for group in range(1, shards):
+        found = found | (ahead == group * narrow)
+    return one_hot(found & (lane < narrow))
+
+
+def pack_local(local, narrow, ratio):
+    vectors = [local[i].reshape(1, narrow) for i in NARROW] + [local[WIDE].reshape(ratio, narrow)]
+    block = jnp.concatenate(vectors, axis=0)
+    return jnp.pad(block, ((0, SLOTS - block.shape[0]), (0, LANES - narrow)))
+
+
+def layer_kernel(shards, gather_cross, scatter_cross, *refs):
+    chips, count = shards // 2, 7
+    refs = list(refs)
+
+    def take(number):
+        taken = refs[:number]
+        del refs[:number]
+        return taken
+
+    frames, cotangent = take(2)
+    ins = take(count)
+    result, d_start = take(2)
+    outs = take(count)
+    weights, terms, held, arrived, others = (take(count) for _ in range(5))
+    found = take(sum(1 for cross in scatter_cross if cross))
+    peers = [found.pop(0) if cross else None for cross in scatter_cross]
+    (
+        hat_one,
+        inv_one,
+        first,
+        query,
+        keys,
+        values,
+        probs,
+        context,
+        mixed,
+        hat_two,
+        inv_two,
+        second,
+        active,
+        slope,
+        d_inner,
+        total,
+        d_context,
+        vec,
+        gvec,
+        place,
+    ) = take(20)
+    gather_sems, scatter_sems = take(7), take(8)
+    frame_count, width = frames.shape
+    hidden = slope.shape[1]
+    ratio, narrow = hidden // width, width // shards
+    ring = Ring(chips)
+    gather = Gather(ring, chips, ins, weights, gather_cross, gather_sems)
+    scatter = Scatter(
+        ring, chips, terms, outs, held, arrived, peers, others, scatter_cross, scatter_sems
+    )
+    greet(ring, (ring.next(), ring.previous(), ring.mate), 2)
+
+    early, late = (PACK, Q, K, V), (O, INNER)
+
+    def hops(group, step):
+        if 1 <= step < chips:
+            for i in group:
+                gather.hop(i, step)
+
+    def crosses(group, step):
+        if 1 <= step < chips:
+            for i in group:
+                gather.cross(i, step)
+
+    def row(name):
+        return vec[VECTOR[name] : VECTOR[name] + 1, :]
+
+    def by_blocks(step):
+        def go(block, carry):
+            step(pl.ds(pl.multiple_of(block * BLOCK, BLOCK), BLOCK))
+            return carry
+
+        lax.fori_loop(0, frame_count // BLOCK, go, 0)
+
+    def by_columns(start, stop, step, size=CHUNK):
+        def go(chunk, carry):
+            step(chunk)
+            return carry
+
+        lax.fori_loop(start, stop, go, 0)
+
+    def columns(chunk, size=CHUNK):
+        return pl.ds(pl.multiple_of(chunk * size, size), size)
+
+    def add_row(index, value):
+        gvec[index : index + 1, :] += value
+
+    def sum_rows(value):
+        return jnp.sum(value, axis=0, keepdims=True)
+
+    for i in early:
+        gather.start(i)
+    for i in late:
+        gather.start(i)
+
+    gvec[...] = jnp.zeros_like(gvec)
+    place[...] = place_table(shards, narrow, width)
+
+    def start_norm(at):
+        value = frames[at, :].astype(jnp.float32)
+        centered = value - jnp.mean(value, axis=-1, keepdims=True)
+        inv = lax.rsqrt(jnp.mean(centered * centered, axis=-1, keepdims=True) + EPSILON)
+        inv_one[at, :] = inv
+        hat_one[at, :] = centered * inv
+        add_row(VECTOR[14], sum_rows(cotangent[at, :].astype(jnp.float32)))
+
+    by_blocks(start_norm)
+
+    for step in range(1, chips):
+        hops(early, step)
+        crosses(early, step - 1)
+        hops(late, step - LAG)
+        crosses(late, step - LAG - 1)
+        if step == 4:
+            gather.start(OUTER)
+    crosses(early, chips - 1)
+    for i in early:
+        gather.finish(i)
+
+    picks = pick_table(shards, ratio)
+    spread = dot_nt(weights[PACK][...], place[...])
+    spread = jnp.where(group_mask(shards, ratio, narrow, width), spread, 0.0)
+    vec[...] = matmul(picks, spread.astype(jnp.bfloat16))
+
+    queue = []
+
+    def serve(number):
+        for _ in range(min(number, len(queue))):
+            queue.pop(0)()
+
+    def later(call, *args):
+        queue.append(functools.partial(call, *args))
+
+    steps = range(1, chips)
+    for step in range(chips - LAG, chips + 1):
+        later(hops, late, step)
+        later(crosses, late, step - 1)
+    for step in range(1, chips + 1):
+        later(hops, (OUTER,), step)
+        later(crosses, (OUTER,), step - 1)
+
+    def first_norm(at):
+        value = hat_one[at, :] * row(0) + row(1)
+        first[at, :] = value.astype(jnp.bfloat16)
+
+    by_blocks(first_norm)
+
+    def project(i, target, bias, scale):
+        def go(chunk):
+            at = columns(chunk)
+            value = matmul(first[...], weights[i][:, at])
+            if bias is not None:
+                value = value + vec[VECTOR[bias] : VECTOR[bias] + 1, at]
+            target[:, at] = (value * scale).astype(jnp.bfloat16)
+
+        by_columns(0, width // CHUNK, go)
+
+    project(Q, query, 3, HD ** (-0.5))
+    serve(2)
+    project(K, keys, None, 1.0)
+    serve(2)
+    project(V, values, 6, 1.0)
+    serve(2)
+
+    pair_width = 2 * HD
+    pairs = width // pair_width
+    lower = iota((1, pair_width), 1) < HD
+    halves = (one_hot(lower), one_hot(jnp.logical_not(lower)))
+
+    def attend(pair):
+        at = pl.ds(pair * pair_width, pair_width)
+        q_pair, k_pair, v_pair = query[:, at], keys[:, at], values[:, at]
+        parts = []
+        for half in range(2):
+            scores = dot_nt(q_pair * halves[half], k_pair)
+            grown = jnp.exp(scores - jnp.max(scores, axis=-1, keepdims=True))
+            prob = (grown / jnp.sum(grown, axis=-1, keepdims=True)).astype(jnp.bfloat16)
+            probs[2 * pair + half] = prob
+            parts.append(matmul(prob, v_pair))
+        context[:, at] = jnp.where(lower, parts[0], parts[1]).astype(jnp.bfloat16)
+
+    for pair in range(pairs):
+        attend(pair)
+        serve(2)
+    while len(queue) > 2 * chips:
+        serve(1)
+
+    for i in late:
+        gather.finish(i)
+
+    def mix(chunk):
+        at = columns(chunk)
+        value = matmul(context[...], weights[O][:, at])
+        bias = vec[VECTOR[8] : VECTOR[8] + 1, at]
+        mixed[:, at] = frames[:, at].astype(jnp.float32) + value + bias
+
+    by_columns(0, width // CHUNK, mix)
+
+    def second_norm(at):
+        value = mixed[at, :]
+        centered = value - jnp.mean(value, axis=-1, keepdims=True)
+        inv = lax.rsqrt(jnp.mean(centered * centered, axis=-1, keepdims=True) + EPSILON)
+        hat = centered * inv
+        inv_two[at, :] = inv
+        hat_two[at, :] = hat
+        second[at, :] = (hat * row(9) + row(10)).astype(jnp.bfloat16)
+
+    by_blocks(second_norm)
+    serve(2)
+
+    per_row = width // CHUNK
+
+    def inner_step(line, chunk):
+        inside = columns(chunk)
+        at = columns(line * per_row + chunk)
+        value = matmul(second[...], weights[INNER][:, at])
+        value = value + vec[SPREAD + line : SPREAD + line + 1, inside]
+        gelu, grad = gelu_parts(value)
+        active[:, at] = gelu.astype(jnp.bfloat16)
+        slope[:, at] = grad.astype(jnp.bfloat16)
+
+    for line in range(ratio):
+        by_columns(0, per_row, functools.partial(inner_step, line))
+        serve(2)
+
+    def outer_grad(chunk):
+        at = columns(chunk)
+        terms[OUTER][at, :] = dot_tn(active[:, at], cotangent[...]).astype(jnp.bfloat16)
+
+    for line in range(ratio):
+        by_columns(line * per_row, (line + 1) * per_row, outer_grad)
+        serve(2)
+    scatter.start(OUTER)
+    serve(len(queue))
+    gather.finish(OUTER)
+
+    def plan(group):
+        for i in group:
+            later(scatter.give, i, 0)
+        for step in range(chips):
+            for i in group:
+                if step + 1 < chips:
+                    later(scatter.give, i, step + 1)
+                later(scatter.hop, i, step)
+
+    def inner_grad(line, chunk):
+        inside = columns(chunk)
+        at = columns(line * per_row + chunk)
+        value = dot_nt(cotangent[...], weights[OUTER][at, :]) * slope[:, at].astype(jnp.float32)
+        gvec[SPREAD + line : SPREAD + line + 1, inside] = sum_rows(value)
+        low = value.astype(jnp.bfloat16)
+        d_inner[:, at] = low
+        terms[INNER][:, at] = dot_tn(second[...], low).astype(jnp.bfloat16)
+
+    plan((OUTER,))
+    for line in range(ratio):
+        by_columns(0, per_row, functools.partial(inner_grad, line))
+        serve(2)
+    scatter.start(INNER)
+    plan((INNER,))
+
+    def second_back(chunk):
+        at = columns(chunk)
+        total[:, at] = dot_nt(d_inner[...], weights[INNER][at, :])
+
+    by_columns(0, width // CHUNK, second_back)
+    serve(2)
+
+    def norm_step(grad_ref, hat_ref, inv_ref, gain, shift, at):
+        grad, hat = grad_ref[at, :], hat_ref[at, :]
+        add_row(VECTOR[gain], sum_rows(grad * hat))
+        add_row(VECTOR[shift], sum_rows(grad))
+        return norm_back(grad, hat, inv_ref[at, :], row(gain))
+
+    def mixed_back(at):
+        back = norm_step(total, hat_two, inv_two, 9, 10, at)
+        value = cotangent[at, :].astype(jnp.float32) + back
+        add_row(VECTOR[8], sum_rows(value))
+        total[at, :] = value
+        second[at, :] = value.astype(jnp.bfloat16)
+
+    by_blocks(mixed_back)
+    serve(2)
+
+    def context_back(chunk):
+        at = columns(chunk)
+        d_context[:, at] = dot_nt(second[...], weights[O][at, :]).astype(jnp.bfloat16)
+
+    by_columns(0, width // CHUNK, context_back)
+    serve(2)
+
+    def square_grad(i, left, right, chunk):
+        at = columns(chunk)
+        terms[i][at, :] = dot_tn(left[:, at], right[...]).astype(jnp.bfloat16)
+
+    def grad_of(i, left, right):
+        by_columns(0, width // CHUNK, functools.partial(square_grad, i, left, right))
+        scatter.start(i)
+
+    grad_of(O, context, second)
+    plan((O,))
+    serve(2)
+
+    def attend_back(pair):
+        at = pl.ds(pair * pair_width, pair_width)
+        q_pair, k_pair, v_pair = query[:, at], keys[:, at], values[:, at]
+        d_pair = d_context[:, at]
+        product = d_pair.astype(jnp.float32) * context[:, at].astype(jnp.float32)
+        d_q, d_k, d_v = [], [], []
+        for half in range(2):
+            prob = probs[2 * pair + half]
+            inside = lower if half == 0 else jnp.logical_not(lower)
+            delta = jnp.sum(jnp.where(inside, product, 0.0), axis=-1, keepdims=True)
+            d_prob = dot_nt(d_pair * halves[half], v_pair)
+            d_score = (prob.astype(jnp.float32) * (d_prob - delta)).astype(jnp.bfloat16)
+            d_v.append(dot_tn(prob, d_pair))
+            d_q.append(matmul(d_score, k_pair))
+            d_k.append(dot_tn(d_score, q_pair))
+        d_query = jnp.where(lower, d_q[0], d_q[1]) * HD ** (-0.5)
+        d_values = jnp.where(lower, d_v[0], d_v[1])
+        gvec[VECTOR[3] : VECTOR[3] + 1, at] = sum_rows(d_query)
+        gvec[VECTOR[6] : VECTOR[6] + 1, at] = sum_rows(d_values)
+        query[:, at] = d_query.astype(jnp.bfloat16)
+        keys[:, at] = jnp.where(lower, d_k[0], d_k[1]).astype(jnp.bfloat16)
+        values[:, at] = d_values.astype(jnp.bfloat16)
+
+    for pair in range(pairs):
+        attend_back(pair)
+        serve(3)
+    grad_of(V, first, values)
+    serve(2)
+    grad_of(K, first, keys)
+    serve(2)
+    grad_of(Q, first, query)
+    serve(2)
+
+    def first_back(chunk):
+        at = columns(chunk)
+        hat_two[:, at] = (
+            dot_nt(query[...], weights[Q][at, :])
+            + dot_nt(keys[...], weights[K][at, :])
+            + dot_nt(values[...], weights[V][at, :])
+        )
+
+    by_columns(0, width // CHUNK, first_back)
+    serve(2)
+
+    def start_back(at):
+        back = norm_step(hat_two, hat_one, inv_one, 0, 1, at)
+        d_start[at, :] = (total[at, :] + back).astype(jnp.bfloat16)
+
+    by_blocks(start_back)
+    lines = dot_tn(picks, gvec[...].astype(jnp.bfloat16))
+    lines = jnp.where(group_mask(shards, ratio, narrow, width), lines, 0.0)
+    terms[PACK][...] = matmul(lines.astype(jnp.bfloat16), place[...]).astype(jnp.bfloat16)
+    scatter.start(PACK)
+    plan((V, K, Q, PACK))
+    serve(8)
+
+    def finish_result(chunk):
+        at = columns(chunk)
+        value = mixed[:, at] + matmul(active[...], weights[OUTER][:, at])
+        bias = vec[VECTOR[14] : VECTOR[14] + 1, at]
+        result[:, at] = (value + bias).astype(jnp.bfloat16)
+
+    by_columns(0, width // CHUNK, finish_result)
+    serve(len(queue))
+    for i in (OUTER, INNER, O, V, K, Q, PACK):
+        scatter.finish(i)
+    for i in range(count):
+        gather.drain(i)
+        scatter.drain(i)
+
+
+LAG = 2
+
+
+def crossings(sizes, names, share):
+    cut = [size // share for size in sizes]
+    return tuple(c if i in names and c % SUBLANES == 0 else 0 for i, c in enumerate(cut))
+
+
+def layer(frames, cotangent, pieces, shards):
+    chips, (rows, width) = shards // 2, frames.shape
+    hidden = pieces[INNER].shape[1]
+    sizes = [piece.shape[0] for piece in pieces]
+    wides = [piece.shape[1] for piece in pieces]
+    gather_cross = crossings(sizes, range(6), 3)
+    thirds = crossings(sizes, (V, O, INNER), 3)
+    quarters = crossings(sizes, (OUTER,), 4)
+    scatter_cross = tuple(a + b for a, b in zip(thirds, quarters))
+    full = [(size * shards, wide) for size, wide in zip(sizes, wides)]
+    ringed = [(size - cross, wide) for size, cross, wide in zip(sizes, scatter_cross, wides)]
+    low, high = jnp.bfloat16, jnp.float32
+    dma = pltpu.SemaphoreType.DMA
+    scratch = (
+        [pltpu.VMEM(shape, low) for shape in full] * 2
+        + [pltpu.VMEM((chips, size, wide), low) for size, wide in zip(sizes, wides)]
+        + [pltpu.VMEM((chips - 1,) + shape, low) for shape in ringed]
+        + [pltpu.VMEM(shape, low) for shape in ringed]
+        + [
+            pltpu.VMEM((chips, cross, wide), low)
+            for cross, wide in zip(scatter_cross, wides)
+            if cross
+        ]
+        + [
+            pltpu.VMEM((rows, width), high),
+            pltpu.VMEM((rows, 1), high),
+            pltpu.VMEM((rows, width), low),
+            pltpu.VMEM((rows, width), low),
+            pltpu.VMEM((rows, width), low),
+            pltpu.VMEM((rows, width), low),
+            pltpu.VMEM((width // HD, rows, rows), low),
+            pltpu.VMEM((rows, width), low),
+            pltpu.VMEM((rows, width), high),
+            pltpu.VMEM((rows, width), high),
+            pltpu.VMEM((rows, 1), high),
+            pltpu.VMEM((rows, width), low),
+            pltpu.VMEM((rows, hidden), low),
+            pltpu.VMEM((rows, hidden), low),
+            pltpu.VMEM((rows, hidden), low),
+            pltpu.VMEM((rows, width), high),
+            pltpu.VMEM((rows, width), low),
+            pltpu.VMEM((SLOTS, width), high),
+            pltpu.VMEM((SLOTS, width), high),
+            pltpu.VMEM((width, LANES), low),
+        ]
+        + [dma((chips, 7))] * 6
+        + [dma((7,))]
+        + [dma((chips, 7))] * 6
+        + [dma((7,))] * 2
+    )
+    vmem = pl.BlockSpec(memory_space=pltpu.VMEM)
+    return pl.pallas_call(
+        functools.partial(layer_kernel, shards, gather_cross, scatter_cross),
+        out_shape=[jax.ShapeDtypeStruct((rows, width), low)] * 2
+        + [jax.ShapeDtypeStruct(shape, high) for shape in zip(sizes, wides)],
+        in_specs=[vmem] * 2 + [pl.BlockSpec(memory_space=pl.ANY)] * 7,
+        out_specs=[vmem] * 9,
+        scratch_shapes=scratch,
+        compiler_params=pltpu.CompilerParams(
+            collective_id=2, has_side_effects=True, vmem_limit_bytes=67043328
+        ),
+        name="layer",
+    )(frames, cotangent, *pieces)
+
+
+def fits(shards, reps, frames, local):
+    narrow, wide = local[0].shape[0], local[WIDE].shape[0]
+    return (
+        reps == 2
+        and shards >= 4
+        and shards & (shards - 1) == 0
+        and frames.shape[0] == 1
+        and frames.shape[1] % CHUNK == 0
+        and frames.shape[2] % CHUNK == 0
+        and all(local[i].shape[0] % (3 * SUBLANES) == 0 for i in WEIGHTS)
+        and wide % narrow == 0
+        and SPREAD + wide // narrow <= SLOTS
+        and narrow <= LANES
+    )
+
+
+def per_device(shards, reps, frames, cotangent, *local):
+    if not fits(shards, reps, frames, local):
+        return per_device_plain(shards, reps, frames, cotangent, *local)
+    narrow, wide = local[0].shape[0], local[WIDE].shape[0]
+    ratio = wide // narrow
+    pieces = [local[i] for i in WEIGHTS] + [pack_local(local, narrow, ratio)]
+    result, d_start, *sums = layer(frames[0], cotangent[0], pieces, shards)
+    out = [None] * len(local)
+    for k, i in enumerate(WEIGHTS):
+        out[i] = sums[k]
+    for k, i in enumerate(NARROW):
+        out[i] = sums[PACK][k, :narrow]
+    out[WIDE] = sums[PACK][SPREAD : SPREAD + ratio, :narrow].reshape(-1)
+    return (result[None], d_start[None], *out)
 
 
 def solution(mesh):

time: 264 us -> 252 us (0.955)
  Pallas kernels: 170 us -> 239 us
  matrix products: 43 us -> 0 us
  local copies, waits for them, and re-layouts: 36.6 us -> 11.7 us
  other arithmetic: 12.2 us -> 0 us
    pallas_call x2 -> x1, Pallas kernels: 170 us -> 239 us  [layer(): pl.pallas_call(functools.partial(layer_kernel, shards, gather_cross, scat...]
    dot_general x24 -> x0, matrix products: 43 us -> none  [the longest x18 35.7 us: matmul(): return jnp.dot(left, right, preferred_element_type=jnp.float32)]
    convert_element_type x21 -> x0, local copies, waits for them, and re-layouts: 16.1 us -> none  [the longest x8 7.8 us: per_device(): low = [total.astype(jnp.bfloat16) for total in totals]]
    reduce_sum x8 -> x0, other arithmetic: 8.09 us -> none  [the longest x1 2.41 us: backward_clip(): g_output_bias = jnp.sum(d_mixed, axis=0)]
    unnamed x112 -> x42, local copies, waits for them, and re-layouts: 12.5 us -> 9.74 us
where the time goes in v1:
time: 252 us
  Pallas kernels  239 us (95%)
  local copies, waits for them, and re-layouts  11.7 us (5%)
    pallas_call x1, Pallas kernels, layer(): pl.pallas_call(functools.partial(layer_kernel, shards, gather_cross, scat...  239 us
    unnamed x42, local copies, waits for them, and re-layouts  9.74 us

profile of v1, /device:TPU:0, one launch (start us, length us, event | category | flops | bytes accessed | tf_op | source)
XLA Modules:
  0.0 251.9 jit_solution(9752627526644810547)
XLA Ops:
  0.7 0.0 copy-start.16
  0.7 0.0 copy-start.15
  0.7 0.0 copy-start.11
  0.7 0.0 copy-start.12
  0.7 0.0 copy-start.13
  0.7 0.0 copy-start.14
  0.7 0.6 copy-done.16
  1.3 0.0 copy-start.8
  1.3 0.0 copy-start.9
  1.3 0.0 copy-start.10
  1.3 0.1 reshape.72
  1.4 0.0 copy-done.15
  1.4 0.0 copy-done.11
  1.4 0.0 copy-done.12
  1.4 0.0 copy-done.13
  1.4 0.0 copy-done.14
  1.4 0.5 copy-done.8
  2.0 0.0 copy-done.9
  2.0 0.0 copy-done.10
  2.0 0.1 concatenate.3
  2.1 0.6 pad.4.refs_8_
  2.7 239.4 %layer.1 = (bf16[256,768]{1,0:T(8,128)(2,1)}, bf16[256,768]{1,0:T(8,128)(2,1)}, f32[48,768]{1,0:T(8,128)}, f32[48,768]{1,0:T(8,128)}, f32[48,768]{1,0:T(8,128)},...) custom-call(bf16[256,768]{1,0:T(8,128)(2,1)} %bitcast.30, ...), custom_call_target="tpu_custom_call" | custom-call | tf_op jit(solution)/shard_map/layer/pallas_call | solution.py:1281
  242.1 0.0 copy-start.7
  242.1 0.7 copy-done.7
  242.8 0.5 slice_bitcast_fusion
  243.3 0.6 reshape.73
  244.0 0.0 copy-start.2
  244.0 1.8 copy.42
  245.8 0.0 copy-done.2
  245.8 0.0 copy-start.6
  245.8 0.0 copy-start.5
  245.8 0.0 copy-start.4
  245.8 0.7 copy.43
  246.6 0.2 copy-done.6
  246.8 0.0 copy-start.1
  246.8 0.7 copy.44
  247.5 0.0 copy-done.5
  247.5 0.7 copy.45
  248.1 0.0 copy-done.4
  248.2 0.0 copy-start.3
  248.2 0.7 copy.46
  248.8 0.3 copy-done.3
  249.1 0.7 copy.47
  249.8 0.0 copy-done.1
  249.8 0.0 copy-start
  249.8 0.8 copy.48
  250.6 0.5 copy-done
  251.1 0.8 copy.49
  (1 shorter events, 0.0 us)
Async XLA Ops:
  0.7 0.7 copy-start.16
  0.7 0.7 copy-start.15
  0.7 0.7 copy-start.11
  0.7 0.7 copy-start.12
  0.7 0.7 copy-start.13
  0.7 0.7 copy-start.14
  1.3 0.7 copy-start.8
  1.3 0.7 copy-start.9
  1.3 0.7 copy-start.10
  242.1 0.7 copy-start.7
  244.0 1.8 copy-start.2
  245.8 1.0 copy-start.6
  245.8 1.7 copy-start.5
  245.8 2.3 copy-start.4
  246.8 3.0 %copy-start.1 = (f32[48,3072]{1,0:T(8,128)S(1)}, f32[48,3072]{1,0:T(8,128)}, u32[]{:S(2)}) copy-start(f32[48,3072]{1,0:T(8,128)} %get-tuple-element.73) | copy-start | bytes 1769476
  248.2 1.0 copy-start.3
  249.8 1.3 copy-start

commit v2 on v1

--- a/solution.py
+++ b/solution.py
@@ -935,10 +935,17 @@
     def sum_rows(value):
         return jnp.sum(value, axis=0, keepdims=True)
 
-    for i in early:
-        gather.start(i)
-    for i in late:
-        gather.start(i)
+    groups = ((early, 0), (late, LAG_LATE), ((OUTER,), LAG_OUTER))
+
+    def gather_tick(tick):
+        for group, lag in groups:
+            if tick == lag:
+                for i in group:
+                    gather.start(i)
+            hops(group, tick - lag)
+            crosses(group, tick - lag - 1)
+
+    gather_tick(0)
 
     gvec[...] = jnp.zeros_like(gvec)
     place[...] = place_table(shards, narrow, width)
@@ -953,14 +960,8 @@
 
     by_blocks(start_norm)
 
-    for step in range(1, chips):
-        hops(early, step)
-        crosses(early, step - 1)
-        hops(late, step - LAG)
-        crosses(late, step - LAG - 1)
-        if step == 4:
-            gather.start(OUTER)
-    crosses(early, chips - 1)
+    for tick in range(1, chips + 1):
+        gather_tick(tick)
     for i in early:
         gather.finish(i)
 
@@ -969,22 +970,23 @@
     spread = jnp.where(group_mask(shards, ratio, narrow, width), spread, 0.0)
     vec[...] = matmul(picks, spread.astype(jnp.bfloat16))
 
-    queue = []
+    ticks = [functools.partial(gather_tick, t) for t in range(chips + 1, chips + LAG_OUTER + 1)]
+    late_ticks = LAG_LATE
+    served = [0]
+
+    def serve_gather(number):
+        for _ in range(number):
+            if served[0] < len(ticks):
+                ticks[served[0]]()
+                served[0] += 1
+
+    streams = []
 
     def serve(number):
-        for _ in range(min(number, len(queue))):
-            queue.pop(0)()
-
-    def later(call, *args):
-        queue.append(functools.partial(call, *args))
-
-    steps = range(1, chips)
-    for step in range(chips - LAG, chips + 1):
-        later(hops, late, step)
-        later(crosses, late, step - 1)
-    for step in range(1, chips + 1):
-        later(hops, (OUTER,), step)
-        later(crosses, (OUTER,), step - 1)
+        for _ in range(number):
+            for stream in streams:
+                if stream:
+                    stream.pop(0)()
 
     def first_norm(at):
         value = hat_one[at, :] * row(0) + row(1)
@@ -1003,11 +1005,11 @@
         by_columns(0, width // CHUNK, go)
 
     project(Q, query, 3, HD ** (-0.5))
-    serve(2)
+    serve_gather(SERVE[0])
     project(K, keys, None, 1.0)
-    serve(2)
+    serve_gather(SERVE[1])
     project(V, values, 6, 1.0)
-    serve(2)
+    serve_gather(SERVE[2])
 
     pair_width = 2 * HD
     pairs = width // pair_width
@@ -1028,10 +1030,8 @@
 
     for pair in range(pairs):
         attend(pair)
-        serve(2)
-    while len(queue) > 2 * chips:
-        serve(1)
-
+        serve_gather(pair % 2)
+    serve_gather(late_ticks - served[0])
     for i in late:
         gather.finish(i)
 
@@ -1053,7 +1053,7 @@
         second[at, :] = (hat * row(9) + row(10)).astype(jnp.bfloat16)
 
     by_blocks(second_norm)
-    serve(2)
+    serve_gather(1)
 
     per_row = width // CHUNK
 
@@ -1068,7 +1068,7 @@
 
     for line in range(ratio):
         by_columns(0, per_row, functools.partial(inner_step, line))
-        serve(2)
+        serve_gather(1)
 
     def outer_grad(chunk):
         at = columns(chunk)
@@ -1076,19 +1076,24 @@
 
     for line in range(ratio):
         by_columns(line * per_row, (line + 1) * per_row, outer_grad)
-        serve(2)
+        serve_gather(1)
     scatter.start(OUTER)
-    serve(len(queue))
+    serve_gather(len(ticks))
     gather.finish(OUTER)
 
+    def scatter_tick(group, step):
+        for i in group:
+            if step == 0:
+                scatter.give(i, 0)
+            if step + 1 < chips:
+                scatter.give(i, step + 1)
+            scatter.hop(i, step)
+
     def plan(group):
-        for i in group:
-            later(scatter.give, i, 0)
-        for step in range(chips):
-            for i in group:
-                if step + 1 < chips:
-                    later(scatter.give, i, step + 1)
-                later(scatter.hop, i, step)
+        streams.append([functools.partial(scatter_tick, group, t) for t in range(chips)])
+
+    def waiting():
+        return max(len(stream) for stream in streams)
 
     def inner_grad(line, chunk):
         inside = columns(chunk)
@@ -1102,7 +1107,7 @@
     plan((OUTER,))
     for line in range(ratio):
         by_columns(0, per_row, functools.partial(inner_grad, line))
-        serve(2)
+        serve(PACE_INNER[line % len(PACE_INNER)])
     scatter.start(INNER)
     plan((INNER,))
 
@@ -1111,7 +1116,7 @@
         total[:, at] = dot_nt(d_inner[...], weights[INNER][at, :])
 
     by_columns(0, width // CHUNK, second_back)
-    serve(2)
+    serve(PACE[0])
 
     def norm_step(grad_ref, hat_ref, inv_ref, gain, shift, at):
         grad, hat = grad_ref[at, :], hat_ref[at, :]
@@ -1127,14 +1132,14 @@
         second[at, :] = value.astype(jnp.bfloat16)
 
     by_blocks(mixed_back)
-    serve(2)
+    serve(PACE[1])
 
     def context_back(chunk):
         at = columns(chunk)
         d_context[:, at] = dot_nt(second[...], weights[O][at, :]).astype(jnp.bfloat16)
 
     by_columns(0, width // CHUNK, context_back)
-    serve(2)
+    serve(PACE[2])
 
     def square_grad(i, left, right, chunk):
         at = columns(chunk)
@@ -1146,7 +1151,7 @@
 
     grad_of(O, context, second)
     plan((O,))
-    serve(2)
+    serve(PACE[3])
 
     def attend_back(pair):
         at = pl.ds(pair * pair_width, pair_width)
@@ -1173,13 +1178,16 @@
 
     for pair in range(pairs):
         attend_back(pair)
-        serve(3)
+        serve(PACE_PAIR[pair % len(PACE_PAIR)])
     grad_of(V, first, values)
-    serve(2)
+    plan((V,))
+    serve(PACE[4])
     grad_of(K, first, keys)
-    serve(2)
+    plan((K,))
+    serve(PACE[5])
     grad_of(Q, first, query)
-    serve(2)
+    plan((Q,))
+    serve(PACE[6])
 
     def first_back(chunk):
         at = columns(chunk)
@@ -1190,7 +1198,7 @@
         )
 
     by_columns(0, width // CHUNK, first_back)
-    serve(2)
+    serve(PACE[7])
 
     def start_back(at):
         back = norm_step(hat_two, hat_one, inv_one, 0, 1, at)
@@ -1201,8 +1209,8 @@
     lines = jnp.where(group_mask(shards, ratio, narrow, width), lines, 0.0)
     terms[PACK][...] = matmul(lines.astype(jnp.bfloat16), place[...]).astype(jnp.bfloat16)
     scatter.start(PACK)
-    plan((V, K, Q, PACK))
-    serve(8)
+    plan((PACK,))
+    serve(PACE[8])
 
     def finish_result(chunk):
         at = columns(chunk)
@@ -1211,7 +1219,7 @@
         result[:, at] = (value + bias).astype(jnp.bfloat16)
 
     by_columns(0, width // CHUNK, finish_result)
-    serve(len(queue))
+    serve(waiting())
     for i in (OUTER, INNER, O, V, K, Q, PACK):
         scatter.finish(i)
     for i in range(count):
@@ -1219,7 +1227,12 @@
         scatter.drain(i)
 
 
-LAG = 2
+LAG_LATE = 0
+LAG_OUTER = 2
+SERVE = (1, 1, 1)
+PACE_INNER = (0, 1)
+PACE = (0, 0, 1, 0, 0, 0, 0, 1, 0)
+PACE_PAIR = (0, 0, 1)
 
 
 def crossings(sizes, names, share):

time: 252 us -> 180 us (0.71)
  Pallas kernels: 239 us -> 167 us
    pallas_call x1, Pallas kernels: 239 us -> 167 us  [layer(): pl.pallas_call(functools.partial(layer_kernel, shards, gather_cross, scat...]
where the time goes in v2:
time: 180 us
  Pallas kernels  167 us (93%)
  local copies, waits for them, and re-layouts  11.7 us (6%)
    pallas_call x1, Pallas kernels, layer(): pl.pallas_call(functools.partial(layer_kernel, shards, gather_cross, scat...  167 us
    unnamed x42, local copies, waits for them, and re-layouts  9.74 us

profile of v2, /device:TPU:0, one launch (start us, length us, event | category | flops | bytes accessed | tf_op | source)
XLA Modules:
  0.0 179.5 jit_solution(14782617910037283150)
XLA Ops:
  0.7 0.0 copy-start.16
  0.7 0.0 copy-start.15
  0.7 0.0 copy-start.11
  0.7 0.0 copy-start.12
  0.7 0.0 copy-start.13
  0.7 0.0 copy-start.14
  0.7 0.6 copy-done.16
  1.3 0.0 copy-start.8
  1.3 0.0 copy-start.9
  1.3 0.0 copy-start.10
  1.3 0.1 reshape.72
  1.4 0.0 copy-done.15
  1.4 0.0 copy-done.11
  1.4 0.0 copy-done.12
  1.4 0.0 copy-done.13
  1.4 0.0 copy-done.14
  1.4 0.5 copy-done.8
  2.0 0.0 copy-done.9
  2.0 0.0 copy-done.10
  2.0 0.1 concatenate.3
  2.1 0.6 pad.4.refs_8_
  2.7 167.1 %layer.1 = (bf16[256,768]{1,0:T(8,128)(2,1)}, bf16[256,768]{1,0:T(8,128)(2,1)}, f32[48,768]{1,0:T(8,128)}, f32[48,768]{1,0:T(8,128)}, f32[48,768]{1,0:T(8,128)},...) custom-call(bf16[256,768]{1,0:T(8,128)(2,1)} %bitcast.30, ...), custom_call_target="tpu_custom_call" | custom-call | tf_op jit(solution)/shard_map/layer/pallas_call | solution.py:1294
  169.7 0.0 copy-start.7
  169.7 0.7 copy-done.7
  170.4 0.5 slice_bitcast_fusion
  171.0 0.6 reshape.73
  171.6 0.0 copy-start.2
  171.6 1.8 %copy.42 = bf16[1,256,768]{2,1,0:T(8,128)(2,1)} copy(bf16[1,256,768]{2,1,0:T(8,128)(2,1)} %bitcast.29) | data formatting | bytes 786432
  173.4 0.0 copy-done.2
  173.4 0.0 copy-start.6
  173.4 0.0 copy-start.5
  173.4 0.0 copy-start.4
  173.5 0.7 copy.43
  174.2 0.2 copy-done.6
  174.4 0.0 copy-start.1
  174.5 0.7 copy.44
  175.1 0.0 copy-done.5
  175.1 0.7 copy.45
  175.8 0.0 copy-done.4
  175.8 0.0 copy-start.3
  175.8 0.7 copy.46
  176.4 0.3 copy-done.3
  176.7 0.7 copy.47
  177.4 0.0 copy-done.1
  177.4 0.0 copy-start
  177.4 0.8 copy.48
  178.2 0.5 copy-done
  178.7 0.8 copy.49
  (1 shorter events, 0.0 us)
Async XLA Ops:
  0.7 0.7 copy-start.16
  0.7 0.7 copy-start.15
  0.7 0.7 copy-start.11
  0.7 0.7 copy-start.12
  0.7 0.7 copy-start.13
  0.7 0.7 copy-start.14
  1.3 0.7 copy-start.8
  1.3 0.7 copy-start.9
  1.3 0.7 copy-start.10
  169.7 0.7 copy-start.7
  171.6 1.8 %copy-start.2 = (bf16[256,768]{1,0:T(8,128)(2,1)S(1)}, bf16[256,768]{1,0:T(8,128)(2,1)}, u32[]{:S(2)}) copy-start(bf16[256,768]{1,0:T(8,128)(2,1)} %get-tuple-element.27) | copy-start | bytes 1179652
  173.4 1.0 copy-start.6
  173.4 1.7 copy-start.5
  173.4 2.3 %copy-start.4 = (f32[48,768]{1,0:T(8,128)S(1)}, f32[48,768]{1,0:T(8,128)}, u32[]{:S(2)}) copy-start(f32[48,768]{1,0:T(8,128)} %get-tuple-element.67) | copy-start | bytes 442372
  174.4 3.0 %copy-start.1 = (f32[48,3072]{1,0:T(8,128)S(1)}, f32[48,3072]{1,0:T(8,128)}, u32[]{:S(2)}) copy-start(f32[48,3072]{1,0:T(8,128)} %get-tuple-element.73) | copy-start | bytes 1769476
  175.8 1.0 copy-start.3
  177.4 1.3 copy-start
